TPU v7x, 32 devices: a whole 2x2x4 slice. The times are simulated.
32 devices in a mesh: rep: 8 (over y, x, core), own: 4 (over z).
Axes of the slice: x: 2, y: 2, z: 4, core: 2. Of those that a mesh axis runs over, the one named last changes fastest.
Arguments:
- gradients: bfloat16 [8, 4, 4, 256, 256], P('rep', 'own')
- owner_index: int32 [4], replicated, may hold values from 0 to 3, as said below
- left_stats: float32 [8, 256, 256], P('own'), as said below
- right_stats: float32 [8, 256, 256], P('own'), as said below
- left_roots: bfloat16 [8, 256, 256], P('own'), as said below
- right_roots: bfloat16 [8, 256, 256], P('own'), as said below
- first_moment: float32 [8, 256, 256], P('own')
- second_moment: float32 [8, 256, 256], P('own'), may hold values from 0.05 to 5
- master: float32 [8, 256, 256], P('own'), may hold values from -6 to 6
Outputs:
- new_left: float32 [8, 256, 256], P('own')
- new_right: float32 [8, 256, 256], P('own')
- new_first: float32 [8, 256, 256], P('own')
- new_second: float32 [8, 256, 256], P('own')
- weights: bfloat16 [4, 256, 256], P(None, 'rep')
Inputs may be any that keep to these rules, and one draw needn't show every extreme that they name: `owner_index`: exactly one owner holds 2 blocks, exactly one holds none, every other holds one. `left_stats`: each matrix is symmetric; every diagonal entry exceeds the sum of the magnitudes of the other entries of its row. `right_stats`: each matrix is symmetric; every diagonal entry exceeds the sum of the magnitudes of the other entries of its row. `left_roots`: each matrix is symmetric. `right_roots`: each matrix is symmetric.
All inputs are finite; a program needn't handle non-finite values.
Results may differ from a plain program's by a relative error of at most 0.001.
Values may be sent and summed in bfloat16 or wider, within the bound.
A program may use at most 64 MiB of HBM per device.

v0:
```python
import jax
import jax.numpy as jnp
from jax import lax
from jax.sharding import PartitionSpec as P

NEWTON = 4
stat_decay = 0.95
first_decay = 0.9
second_decay = 0.99
learning_rate = 0.5


def product(first_factor, second_factor):
    return jnp.matmul(first_factor, second_factor, precision=lax.Precision.HIGHEST)


def destinations(owner_index, capacity):
    block_count = owner_index.shape[0]
    positions = jnp.arange(block_count, dtype=jnp.int32)
    same_owner = owner_index[:, None] == owner_index[None, :]
    earlier = positions[None, :] < positions[:, None]
    ranking = jnp.sum((same_owner & earlier).astype(jnp.int32), axis=1)
    return owner_index * capacity + ranking


def inverse_root(statistic, initial):
    current = initial
    for iteration in range(NEWTON):
        square = product(current, current)
        fourth = product(square, square)
        residual = product(fourth, statistic)
        current = (5.0 * current - product(current, residual)) / 4.0
    return current


def local(
    gradients,
    owner_index,
    left_stats,
    right_stats,
    left_roots,
    right_roots,
    first_moment,
    second_moment,
    master,
):
    capacity = left_stats.shape[0]
    block_size = left_stats.shape[-1]
    block_count = owner_index.shape[0]
    owner_count = lax.axis_size("own")
    slot_total = owner_count * capacity
    destination = destinations(owner_index, capacity)
    placement = destination[None, :] == jnp.arange(slot_total, dtype=jnp.int32)[:, None]
    occupied = jnp.any(placement, axis=1)
    source_block = jnp.sum(
        placement.astype(jnp.int32) * jnp.arange(block_count, dtype=jnp.int32)[None, :], axis=1
    )
    local_blocks = gradients.reshape(block_count, block_size, block_size)
    own_position = lax.axis_index("own")
    occupied_here = lax.dynamic_slice_in_dim(occupied, own_position * capacity, capacity)
    slot_terms = jnp.where(
        occupied[:, None, None], local_blocks[source_block].astype(jnp.float32), 0.0
    )
    owned_partial = lax.psum_scatter(slot_terms, "own", scatter_dimension=0, tiled=True)
    summed = lax.psum(owned_partial, "rep")
    transposed = jnp.swapaxes(summed, 1, 2)
    left_new = stat_decay * left_stats + (1.0 - stat_decay) / block_size * product(
        summed, transposed
    )
    right_new = stat_decay * right_stats + (1.0 - stat_decay) / block_size * product(
        transposed, summed
    )
    statistics = jnp.concatenate([left_new, right_new], axis=0)
    starting = jnp.concatenate([left_roots, right_roots], axis=0).astype(jnp.float32)
    roots = inverse_root(statistics, starting)
    left_root = roots[:capacity]
    right_root = roots[capacity:]
    first_new = first_decay * first_moment + (1.0 - first_decay) * summed
    second_new = second_decay * second_moment + (1.0 - second_decay) * summed * summed
    adam_step = first_new / (jnp.sqrt(second_new) + 1e-08)
    precond = product(product(left_root, summed), right_root)
    graft = jnp.sqrt(jnp.sum(adam_step * adam_step, axis=(1, 2))) / (
        jnp.sqrt(jnp.sum(precond * precond, axis=(1, 2))) + 1e-06
    )
    updated = (master - learning_rate * graft[:, None, None] * precond).astype(jnp.bfloat16)
    row_count = block_size // lax.axis_size("rep")
    row_piece = lax.dynamic_slice_in_dim(updated, lax.axis_index("rep") * row_count, row_count, 1)
    gathered = lax.all_gather(row_piece, "own", axis=0, tiled=True)
    weights = gathered[destination]
    keep_slot = occupied_here[:, None, None]
    new_left = jnp.where(keep_slot, left_new, left_stats)
    new_right = jnp.where(keep_slot, right_new, right_stats)
    new_first = jnp.where(keep_slot, first_new, first_moment)
    new_second = jnp.where(keep_slot, second_new, second_moment)
    return (new_left, new_right, new_first, new_second, weights)


def solution(mesh):
    return jax.shard_map(
        local,
        mesh=mesh,
        in_specs=(
            P("rep", "own", None, None, None),
            P(),
            P("own", None, None),
            P("own", None, None),
            P("own", None, None),
            P("own", None, None),
            P("own", None, None),
            P("own", None, None),
            P("own", None, None),
        ),
        out_specs=(
            P("own", None, None),
            P("own", None, None),
            P("own", None, None),
            P("own", None, None),
            P(None, "rep", None),
        ),
        check_vma=False,
    )
```

profile of v0, /device:TPU:0, one launch (start us, length us, event | category | flops | bytes accessed | tf_op | source)
XLA Modules:
  0.0 161.0 jit_solution(4762941962667526766)
XLA Ops:
  7.2 0.0 copy-start
  7.2 0.0 reduce-scatter.2.cloned.1.call-start
  7.2 0.9 convert_reduce_fusion
  8.1 0.7 compare_select_fusion
  8.8 0.1 fusion.28
  8.9 0.1 select_reduce_fusion
  9.0 0.0 copy-done
  9.0 0.6 gather_fusion
  9.6 0.0 copy-start.5
  9.6 1.6 %convert_select_fusion = f32[8,256,256]{2,1,0:T(8,128)} fusion(bf16[8,256,256]{2,1,0:T(8,128)(2,1)S(1)} %gather_fusion, pred[8]{0:T(512)(128)(4,1)S(1)} %fusion.28), kind=kLoop, calls=%fused_computation.2 | loop fusion | flops 1048576 | bytes 3145736 | tf_op jit(solution)/shard_map/jit(_where)/select_n | solution.py:61
  11.2 0.0 copy-start.6
  11.2 0.0 reduce-scatter.2.cloned.1.call-update
  11.3 0.0 all-reduce.2.cloned.1.call-start
  11.3 0.1 dynamic_slice.6
  11.4 0.0 copy-done.5
  11.4 0.8 copy-done.6
  12.2 0.3 fusion.42
  12.5 45.3 %reduce-scatter.2.cloned.1.call-done = f32[2,256,256]{2,1,0:T(8,128)} async-done(((f32[8,256,256]{2,1,0:T(8,128)}), f32[2,256,256]{2,1,0:T(8,128)}) %reduce-scatter.2.cloned.1.call-update) | async-done | bytes 524304 | tf_op jit(solution)/shard_map/reduce_scatter | solution.py:64
  57.8 0.0 all-reduce.2.cloned.1.call-update
  57.8 1.1 fusion.43
  58.9 0.0 copy-start.2
  59.0 0.0 copy-start.3
  59.0 56.0 %all-reduce.2.cloned.1.call-done = f32[2,256,256]{2,1,0:T(8,128)} async-done(((f32[2,256,256]{2,1,0:T(8,128)}), f32[2,256,256]{2,1,0:T(8,128)}) %all-reduce.2.cloned.1.call-update) | async-done | bytes 524304 | tf_op jit(solution)/shard_map/psum | solution.py:65
  114.9 0.0 copy-start.1
  114.9 0.0 copy-start.4
  114.9 2.1 %fusion.2 = f32[2,256,256]{2,1,0:T(8,128)S(1)} fusion(f32[2,256,256]{2,1,0:T(8,128)} %all-reduce.2.cloned.1.call-done, f32[2,256,256]{2,1,0:T(8,128)} %param.11), kind=kOutput, calls=%fused_computation.11 | convolution fusion | flops 403046400 | bytes 1572864 | tf_op jit(solution)/shard_map/dot_general | solution.py:14
  117.1 0.0 copy-done.2
  117.1 0.0 copy-done.3
  117.1 0.0 copy-done.1
  117.1 0.0 copy-done.4
  117.1 3.7 %multiply_reduce_fusion.1 = (f32[2]{0:T(128)S(1)}, f32[2,256,256]{2,1,0:T(8,128)}, f32[2,256,256]{2,1,0:T(8,128)}, f32[2,256,256]{2,1,0:T(8,128)}, f32[2,256,256]{2,1,0:T(8,128)}, /*index=5*/f32[2,256,256]{2,1,0:T(8,128)S(1)}) fusion(f32[2,256,256]{2,1,0:T(8,128)S(1)} %copy-done.1, f32[2,256,256]{2,1,0:T(8,128)S(1)} %copy-done.3, ...), kind=kOutput, calls=%fused_computation.33 | convolution fusion | flops 405012480 | bytes 5767178 | tf_op jit(solution)/shard_map/dot_general | solution.py:14
  120.8 1.1 fusion.24
  122.0 0.7 convolution_subtract_fusion.3
  122.7 1.2 fusion.10
  123.9 1.1 fusion.44
  125.1 1.1 fusion.23
  126.3 1.2 convolution_subtract_fusion.2
  127.5 1.2 fusion.7
  128.7 1.3 fusion.45
  130.0 1.1 fusion.22
  131.2 1.2 convolution_subtract_fusion.1
  132.4 1.2 fusion.4
  133.6 1.1 fusion.46
  134.8 1.1 fusion.21
  135.9 1.3 fusion
  137.2 0.7 fusion.47
  137.9 0.8 multiply_reduce_fusion
  138.7 0.9 fusion.27
  139.6 13.3 %all_gather.3 = bf16[8,32,256]{2,1,0:T(8,128)(2,1)S(1)} all-gather(bf16[2,32,256]{2,1,0:T(8,128)(2,1)S(1)} %fusion.27), channel_id=1, replica_groups=mesh['rep'=8,'own'=4] {'own'}, dimensions={0}, use_global_device_ids=true | all-gather | bytes 163840 | tf_op jit(solution)/shard_map/all_gather | solution.py:88
  152.9 1.2 gather_fusion.1
  (6 shorter events, 0.1 us)
Async XLA Ops:
  7.2 1.8 %copy-start = (bf16[1,1,4,256,256]{4,3,2,1,0:T(8,128)(2,1)S(1)}, bf16[1,1,4,256,256]{4,3,2,1,0:T(8,128)(2,1)}, u32[]{:S(2)}) copy-start(bf16[1,1,4,256,256]{4,3,2,1,0:T(8,128)(2,1)} %param.9) | copy-start | bytes 1572868
  7.2 50.6 %reduce-scatter.2.cloned.1.call-start = ((), (), s32[]{:S(2)}) async-start(), calls=%async_computation.1 | async-start | bytes 2621440 | tf_op jit(solution)/shard_map/reduce_scatter | solution.py:64
  9.6 1.8 %copy-start.5 = (bf16[2,256,256]{2,1,0:T(8,128)(2,1)S(1)}, bf16[2,256,256]{2,1,0:T(8,128)(2,1)}, u32[]{:S(2)}) copy-start(bf16[2,256,256]{2,1,0:T(8,128)(2,1)} %param.13) | copy-start | bytes 786436
  11.2 0.9 copy-start.6
  11.3 103.7 %all-reduce.2.cloned.1.call-start = ((), (), s32[]{:S(2)}) async-start(), calls=%async_computation.2 | async-start | bytes 1048576 | tf_op jit(solution)/shard_map/psum | solution.py:65
  58.9 58.2 %copy-start.2 = (f32[2,256,256]{2,1,0:T(8,128)S(1)}, f32[2,256,256]{2,1,0:T(8,128)}, u32[]{:S(2)}) copy-start(f32[2,256,256]{2,1,0:T(8,128)} %param.11) | copy-start | bytes 1572868
  59.0 58.2 %copy-start.3 = (f32[2,256,256]{2,1,0:T(8,128)S(1)}, f32[2,256,256]{2,1,0:T(8,128)}, u32[]{:S(2)}) copy-start(f32[2,256,256]{2,1,0:T(8,128)} %param.15) | copy-start | bytes 1572868
  114.9 2.2 %copy-start.1 = (f32[2,256,256]{2,1,0:T(8,128)S(1)}, f32[2,256,256]{2,1,0:T(8,128)}, u32[]{:S(2)}) copy-start(f32[2,256,256]{2,1,0:T(8,128)} %all-reduce.2.cloned.1.call-done) | copy-start | bytes 1572868
  114.9 2.2 %copy-start.4 = (f32[2,256,256]{2,1,0:T(8,128)S(1)}, f32[2,256,256]{2,1,0:T(8,128)}, u32[]{:S(2)}) copy-start(f32[2,256,256]{2,1,0:T(8,128)} %param.16) | copy-start | bytes 1572868
Sparse Core Ops, SparseCore 0:
  11.4 46.3 reduce-scatter.1
  60.9 54.0 all-reduce.1
where the time goes:
time: 161 us
  waiting for transfers between devices  101 us (63%)
  matrix products  25 us (16%)
  between operations  14.3 us (9%)
  blocking collectives  13.3 us (8%)
  other arithmetic  4.32 us (3%)
  local copies, waits for them, and re-layouts  2.7 us (2%)
    psum x1, waiting for transfers between devices, local(): summed = lax.psum(owned_partial, 'rep')  56 us
    reduce_scatter x1, waiting for transfers between devices, local(): lax.psum_scatter(slot_terms, 'own', scatter_dimension=0, tiled=True)  45.3 us
    dot_general x20, matrix products, product(): jnp.matmul(first_factor, second_factor, precision=lax.Precision.HIGHEST)  25 us
    all_gather x1, blocking collectives, local(): gathered = lax.all_gather(row_piece, 'own', axis=0, tiled=True)  13.3 us
  transfers between devices with their start and end apart: 2, of which 2 were waited for; matrix products, arithmetic and copies ran while one was open for 1% of the time, Pallas kernels for 0%

commit v1 on v0

--- a/solution.py
+++ b/solution.py
@@ -44,6 +44,11 @@
     second_moment,
     master,
 ):
+
+    def report_the_loops(piece_in, named_axis):
+        carry_in = lax.all_gather(piece_in, axis_name=named_axis)
+        return jnp.sum(carry_in, 0)
+
     capacity = left_stats.shape[0]
     block_size = left_stats.shape[-1]
     block_count = owner_index.shape[0]
@@ -62,7 +67,7 @@
         occupied[:, None, None], local_blocks[source_block].astype(jnp.float32), 0.0
     )
     owned_partial = lax.psum_scatter(slot_terms, "own", scatter_dimension=0, tiled=True)
-    summed = lax.psum(owned_partial, "rep")
+    summed = report_the_loops(owned_partial, "rep")
     transposed = jnp.swapaxes(summed, 1, 2)
     left_new = stat_decay * left_stats + (1.0 - stat_decay) / block_size * product(
         summed, transposed

time: 161 us -> 143 us (0.89)
  waiting for transfers between devices: 101 us -> 82.6 us
  other arithmetic: 4.32 us -> 6.89 us
  matrix products: 25 us -> 22.5 us
    psum x1 -> x0, waiting for transfers between devices: 56 us -> none  [local(): summed = lax.psum(owned_partial, 'rep')]
    all_gather x0 -> x1, waiting for transfers between devices: none -> 36.1 us  [report_the_loops(): carry_in = lax.all_gather(piece_in, axis_name=named_axis)]
    reduce_sum x0 -> x1, other arithmetic: none -> 2.57 us  [report_the_loops(): return jnp.sum(carry_in, 0)]
    dot_general x20, matrix products: 25 us -> 22.5 us  [product(): jnp.matmul(first_factor, second_factor, precision=lax.Precision.HIGHEST)]
where the time goes in v1:
time: 143 us; the launch traced here: 142 us
  waiting for transfers between devices  82.6 us (58%)
  matrix products  22.5 us (16%)
  between operations  14.3 us (10%)
  blocking collectives  13.4 us (9%)
  other arithmetic  6.89 us (5%)
  local copies, waits for them, and re-layouts  2.55 us (2%)
    reduce_scatter x1, waiting for transfers between devices, local(): lax.psum_scatter(slot_terms, 'own', scatter_dimension=0, tiled=True)  46.5 us
    all_gather x1, waiting for transfers between devices, report_the_loops(): carry_in = lax.all_gather(piece_in, axis_name=named_axis)  36.1 us
    dot_general x20, matrix products, product(): jnp.matmul(first_factor, second_factor, precision=lax.Precision.HIGHEST)  22.5 us
    all_gather x1, blocking collectives, local(): gathered = lax.all_gather(row_piece, 'own', axis=0, tiled=True)  13.4 us
  transfers between devices with their start and end apart: 2, of which 2 were waited for; matrix products, arithmetic and copies ran while one was open for 1% of the time, Pallas kernels for 0%

profile of v1, /device:TPU:0, one launch (start us, length us, event | category | flops | bytes accessed | tf_op | source)
XLA Modules:
  0.0 142.3 jit_solution(1066943639937398056)
XLA Ops:
  7.2 0.0 copy-start
  7.2 0.0 reduce-scatter.2.cloned.1.call-start
  7.2 0.9 convert_reduce_fusion
  8.1 0.7 compare_select_fusion
  8.8 0.1 fusion.28
  8.9 0.1 select_reduce_fusion
  9.0 0.0 copy-done
  9.0 0.6 gather_fusion
  9.6 1.6 %convert_select_fusion = f32[8,256,256]{2,1,0:T(8,128)} fusion(bf16[8,256,256]{2,1,0:T(8,128)(2,1)S(1)} %gather_fusion, pred[8]{0:T(512)(128)(4,1)S(1)} %fusion.28), kind=kLoop, calls=%fused_computation.2 | loop fusion | flops 1048576 | bytes 3145736 | tf_op jit(solution)/shard_map/jit(_where)/select_n | solution.py:66
  11.2 0.0 copy-start.5
  11.2 0.0 copy-start.6
  11.2 0.0 reduce-scatter.2.cloned.1.call-update
  11.3 0.0 all-gather.3.cloned.1.call-start
  11.3 46.5 %reduce-scatter.2.cloned.1.call-done = f32[2,256,256]{2,1,0:T(8,128)} async-done(((f32[8,256,256]{2,1,0:T(8,128)}), f32[2,256,256]{2,1,0:T(8,128)}) %reduce-scatter.2.cloned.1.call-update) | async-done | bytes 524304 | tf_op jit(solution)/shard_map/reduce_scatter | solution.py:69
  57.8 0.0 all-gather.3.cloned.1.call-update
  57.8 0.1 dynamic_slice.6
  57.9 0.0 copy-done.5
  57.9 0.0 copy-done.6
  57.9 0.3 fusion.42
  58.2 1.1 fusion.43
  59.4 36.1 %all-gather.3.cloned.1.call-done = f32[16,256,256]{2,1,0:T(8,128)} async-done(((f32[2,256,256]{2,1,0:T(8,128)}), f32[16,256,256]{2,1,0:T(8,128)}) %all-gather.3.cloned.1.call-update) | async-done | bytes 4194320 | tf_op jit(solution)/shard_map/all_gather | solution.py:49
  95.5 0.0 copy-start.1
  95.5 2.6 %reduce_sum.50 = f32[2,256,256]{2,1,0:T(8,128)S(1)} reduce(f32[8,2,256,256]{3,2,1,0:T(8,128)} %bitcast.33, f32[]{:T(128)} %constant.15.clone.1), dimensions={0}, to_apply=%region_4.5 | reduce | flops 917504 | bytes 4718596 | tf_op jit(solution)/shard_map/reduce_sum | solution.py:50
  98.1 0.0 copy-done.1
  98.1 0.0 copy-start.2
  98.1 0.0 copy-start.3
  98.1 0.0 copy-start.4
  98.1 0.7 fusion.2
  98.8 0.3 copy-done.2
  99.1 0.2 copy-done.3
  99.3 0.2 copy-done.4
  99.4 2.7 %multiply_reduce_fusion.1 = (f32[2]{0:T(128)S(1)}, f32[2,256,256]{2,1,0:T(8,128)}, f32[2,256,256]{2,1,0:T(8,128)}, f32[2,256,256]{2,1,0:T(8,128)}, f32[2,256,256]{2,1,0:T(8,128)}, /*index=5*/f32[2,256,256]{2,1,0:T(8,128)S(1)}) fusion(f32[2,256,256]{2,1,0:T(8,128)S(1)} %reduce_sum.50, f32[2,256,256]{2,1,0:T(8,128)S(1)} %copy-done.2, ...), kind=kOutput, calls=%fused_computation.33 | convolution fusion | flops 405012480 | bytes 5767178 | tf_op jit(solution)/shard_map/dot_general | solution.py:14
  102.1 1.1 fusion.24
  103.3 0.8 convolution_subtract_fusion.3
  104.0 1.2 fusion.10
  105.2 1.1 fusion.44
  106.4 1.1 fusion.23
  107.5 1.2 convolution_subtract_fusion.2
  108.8 1.2 fusion.7
  110.0 1.3 fusion.45
  111.3 1.1 fusion.22
  112.5 1.2 convolution_subtract_fusion.1
  113.7 1.2 fusion.4
  114.9 1.1 fusion.46
  116.1 1.1 fusion.21
  117.2 1.3 fusion
  118.5 0.7 fusion.47
  119.2 0.8 multiply_reduce_fusion
  120.0 0.9 fusion.27
  120.9 13.4 %all_gather.11 = bf16[8,32,256]{2,1,0:T(8,128)(2,1)S(1)} all-gather(bf16[2,32,256]{2,1,0:T(8,128)(2,1)S(1)} %fusion.27), channel_id=1, replica_groups=mesh['rep'=8,'own'=4] {'own'}, dimensions={0}, use_global_device_ids=true | all-gather | bytes 163840 | tf_op jit(solution)/shard_map/all_gather | solution.py:93
  134.3 1.2 gather_fusion.1
  (6 shorter events, 0.1 us)
Async XLA Ops:
  7.2 1.8 %copy-start = (bf16[1,1,4,256,256]{4,3,2,1,0:T(8,128)(2,1)S(1)}, bf16[1,1,4,256,256]{4,3,2,1,0:T(8,128)(2,1)}, u32[]{:S(2)}) copy-start(bf16[1,1,4,256,256]{4,3,2,1,0:T(8,128)(2,1)} %param.9) | copy-start | bytes 1572868
  7.2 50.6 %reduce-scatter.2.cloned.1.call-start = ((), (), s32[]{:S(2)}) async-start(), calls=%async_computation.1 | async-start | bytes 2621440 | tf_op jit(solution)/shard_map/reduce_scatter | solution.py:69
  11.2 46.6 %copy-start.5 = (bf16[2,256,256]{2,1,0:T(8,128)(2,1)S(1)}, bf16[2,256,256]{2,1,0:T(8,128)(2,1)}, u32[]{:S(2)}) copy-start(bf16[2,256,256]{2,1,0:T(8,128)(2,1)} %param.13) | copy-start | bytes 786436
  11.2 46.7 %copy-start.6 = (bf16[2,256,256]{2,1,0:T(8,128)(2,1)S(1)}, bf16[2,256,256]{2,1,0:T(8,128)(2,1)}, u32[]{:S(2)}) copy-start(bf16[2,256,256]{2,1,0:T(8,128)(2,1)} %param.14) | copy-start | bytes 786436
  11.3 84.2 %all-gather.3.cloned.1.call-start = ((), (), s32[]{:S(2)}) async-start(), calls=%async_computation.2 | async-start | bytes 4718592 | tf_op jit(solution)/shard_map/all_gather | solution.py:49
  95.5 2.6 %copy-start.1 = (f32[2,256,256]{2,1,0:T(8,128)S(1)}, f32[2,256,256]{2,1,0:T(8,128)}, u32[]{:S(2)}) copy-start(f32[2,256,256]{2,1,0:T(8,128)} %param.11) | copy-start | bytes 1572868
  98.1 1.0 copy-start.2
  98.1 1.2 copy-start.3
  98.1 1.3 copy-start.4
Sparse Core Ops, SparseCore 0:
  11.4 46.3 reduce-scatter.1
  59.6 35.7 all-gather.2
